TPU v7x, 32 devices: a whole 2x2x4 slice. The times are simulated.
32 devices in a mesh: freq: 4 (over y, x), trace: 8 (over z, core).
Axes of the slice: x: 2, y: 2, z: 4, core: 2. Of those that a mesh axis runs over, the one named last changes fastest.
Arguments:
- traces: float32 [64, 256, 2048], P(('freq', 'trace')), may hold values from -6 to 6
- source_weights: float32 [64, 256, 512], P(None, 'trace'), may hold values from -0.09375 to 0.09375
- level_weights: float32 [3, 2048, 1024], P(None, 'trace'), may hold values from -0.1875 to 0.1875
- slowness_weights: float32 [4096, 512], P('trace'), may hold values from -0.25 to 0.25
Outputs:
- radon_image: float32 [4096, 256], P(('trace', 'freq'))
All inputs are finite; a program needn't handle non-finite values.
Results may differ from a plain program's by a relative error of at most 0.00011.
Values sent between devices are 32-bit elements; how exact they have to be, the bound alone decides.
A program may use at most 128 MiB of HBM per device.

v0:
```python
import math

import jax
import jax.numpy as jnp
from jax import lax
from jax.sharding import PartitionSpec as P

FREQS = 1024
TAUS = 256


EXACT = lax.Precision.HIGHEST


def from_partner(block, axis, apart):
    count = lax.axis_size(axis)
    route = []
    for low in range(count):
        high = low | 1 << apart
        if high != low and high < count:
            route += [(low, high), (high, low)]
    return lax.ppermute(block, axis, route)


def product(left, right):
    return jnp.dot(left, right, precision=EXACT, preferred_element_type=jnp.float32)


def phase_table(rows, columns, period):
    index_grid = (
        jnp.arange(rows, dtype=jnp.int32)[:, None]
        * jnp.arange(columns, dtype=jnp.int32)[None, :]
        % period
    )
    angles = index_grid.astype(jnp.float32) * (2.0 * math.pi / period)
    return (jnp.cos(angles), -jnp.sin(angles))


def time_spectrum(samples, kept):
    row_count, sample_count = samples.shape
    outer = 2 ** ((sample_count.bit_length() - 1) // 2)
    inner = sample_count // outer
    blocks = samples.reshape(row_count, outer, inner)
    first_cos, first_sin = phase_table(outer, outer, outer)
    section_real = jnp.einsum(
        "rmn,mf->rfn", blocks, first_cos, precision=EXACT, preferred_element_type=jnp.float32
    )
    section_imag = jnp.einsum(
        "rmn,mf->rfn", blocks, first_sin, precision=EXACT, preferred_element_type=jnp.float32
    )
    twist_cos, twist_sin = phase_table(outer, inner, sample_count)
    turned_real = section_real * twist_cos - section_imag * twist_sin
    turned_imag = section_real * twist_sin + section_imag * twist_cos
    upper = -(-kept // outer)
    second_cos, second_sin = phase_table(inner, upper, inner)
    final_real = jnp.einsum(
        "rfn,ng->rgf", turned_real, second_cos, precision=EXACT, preferred_element_type=jnp.float32
    ) - jnp.einsum(
        "rfn,ng->rgf", turned_imag, second_sin, precision=EXACT, preferred_element_type=jnp.float32
    )
    final_imag = jnp.einsum(
        "rfn,ng->rgf", turned_real, second_sin, precision=EXACT, preferred_element_type=jnp.float32
    ) + jnp.einsum(
        "rfn,ng->rgf", turned_imag, second_cos, precision=EXACT, preferred_element_type=jnp.float32
    )
    scaled = 1.0 / math.sqrt(sample_count)
    final_real = final_real.reshape(row_count, upper * outer) * scaled
    final_imag = final_imag.reshape(row_count, upper * outer) * scaled
    return (final_real, final_imag)


def body(traces, source_weights, level_weights, slowness_weights):
    freq_count = lax.axis_size("freq")
    trace_count = lax.axis_size("trace")
    shot_dev, offset_count, sample_count = traces.shape
    freq_dev = FREQS // freq_count
    box_offsets = offset_count // trace_count
    coeff_count = source_weights.shape[2] // 2
    freq_ids = jnp.arange(FREQS, dtype=jnp.int32)
    spec_real, spec_imag = time_spectrum(traces.reshape(-1, sample_count), FREQS)
    spec_real = spec_real.reshape(shot_dev, trace_count, box_offsets, freq_count, 1, freq_dev)
    spec_imag = spec_imag.reshape(shot_dev, trace_count, box_offsets, freq_count, 1, freq_dev)
    spectrum = jnp.concatenate([spec_real, spec_imag], axis=4).reshape(
        shot_dev, trace_count, box_offsets, freq_count, 2 * freq_dev
    )
    spectrum = jnp.transpose(spectrum, (0, 3, 1, 2, 4))
    spectrum = spectrum.reshape(shot_dev, freq_count * trace_count, box_offsets, 2 * freq_dev)
    spectrum = lax.all_to_all(spectrum, ("freq", "trace"), split_axis=1, concat_axis=0, tiled=True)
    spectrum = spectrum.reshape(-1, 2 * freq_dev)
    sources = source_weights.reshape(-1, 2 * coeff_count)
    gram = jnp.einsum(
        "xk,xc->kc", sources, spectrum, precision=EXACT, preferred_element_type=jnp.float32
    )
    coeff_real = gram[:coeff_count, :freq_dev] - gram[coeff_count:, freq_dev:]
    coeff_imag = gram[:coeff_count, freq_dev:] + gram[coeff_count:, :freq_dev]
    coeffs = jnp.concatenate([coeff_real, coeff_imag], axis=1)
    for level_no in range(level_weights.shape[0]):
        partner = from_partner(coeffs, "trace", level_no)
        weights = level_weights[level_no]
        stacked = jnp.concatenate([coeffs, partner], axis=0)
        real_rows = product(weights[:, : 2 * coeff_count], stacked)
        imag_rows = product(weights[:, 2 * coeff_count :], stacked)
        coeffs = jnp.concatenate(
            [
                real_rows[:, :freq_dev] - imag_rows[:, freq_dev:],
                real_rows[:, freq_dev:] + imag_rows[:, :freq_dev],
            ],
            axis=1,
        )
    first_terms = product(slowness_weights[:, :coeff_count], coeffs)
    second_terms = product(slowness_weights[:, coeff_count:], coeffs)
    image_real = first_terms[:, :freq_dev] - second_terms[:, freq_dev:]
    image_imag = first_terms[:, freq_dev:] + second_terms[:, :freq_dev]
    tau_ids = jnp.arange(TAUS, dtype=jnp.int32) * (sample_count // (4 * TAUS))
    norm_scale = 1.0 / math.sqrt(FREQS)
    image_both = jnp.stack([image_real, image_imag], axis=1)
    regrouped = lax.all_to_all(image_both, "freq", split_axis=0, concat_axis=2, tiled=True)
    turns = (freq_ids[:, None] * tau_ids[None, :] % sample_count).astype(jnp.float32) * (
        2.0 * math.pi / sample_count
    )
    cosines = jnp.cos(turns)
    sines = jnp.sin(turns)
    radon_image = (product(regrouped[:, 0], cosines) - product(regrouped[:, 1], sines)) * norm_scale
    return radon_image


def solution(mesh):
    return jax.shard_map(
        body,
        mesh=mesh,
        in_specs=(
            P(("freq", "trace"), None, None),
            P(None, "trace", None),
            P(None, "trace", None),
            P("trace", None),
        ),
        out_specs=P(("trace", "freq"), None),
        check_vma=False,
    )
```

profile of v0, /device:TPU:0, one launch (start us, length us, event | category | flops | bytes accessed | tf_op | source)
XLA Modules:
  0.0 287.1 jit_solution(17272750464166523207)
XLA Ops:
  0.1 7.9 %reshape.90 = f32[512,32,64]{2,1,0:T(8,128)} reshape(f32[2,256,2048]{2,1,0:T(8,128)} %param.4) | data formatting | bytes 8388608 | tf_op jit(solution)/shard_map/reshape;reshape | solution.py:43
  8.0 7.7 %copy.68 = f32[512,32,64]{0,1,2:T(8,128)} copy(f32[512,32,64]{2,1,0:T(8,128)} %reshape.90) | data formatting | bytes 8388608 | tf_op jit(solution)/shard_map/reshape;reshape | solution.py:43
  15.7 5.9 %fusion.48 = f32[32,512,64]{1,0,2:T(8,128)S(1)} fusion(f32[512,32,64]{0,1,2:T(8,128)} %copy.68), kind=kOutput, calls=%fused_computation.93 | convolution fusion | flops 402668544 | bytes 8388608 | tf_op jit(solution)/shard_map/rmn,mf->rfn/dot_general | solution.py:48
  21.7 4.8 %subtract_bitcast_fusion = (f32[512,32,64]{0,1,2:T(8,128)S(1)}, f32[512,32,64]{0,1,2:T(8,128)S(1)}) fusion(f32[32,512,64]{1,0,2:T(8,128)S(1)} %fusion.48, f32[32,64]{0,1:T(8,128)S(1)} %get-tuple-element.20, f32[32,64]{0,1:T(8,128)S(1)} %get-tuple-element.21, f32[512,32,64]{0,1,2:T(8,128)S(1)} %copy-done), kind=kOutput, calls=%fused_computation.2 | convolution fusion | flops 408958976 | bytes 16793600 | tf_op jit(solution)/shard_map/rmn,mf->rfn/dot_general | solution.py:45
  26.5 4.6 %fusion.2 = f32[32,512,32]{1,0,2:T(8,128)S(1)} fusion(f32[512,32,64]{0,1,2:T(8,128)S(1)} %get-tuple-element.6), kind=kOutput, calls=%fused_computation.5 | convolution fusion | flops 402683904 | bytes 6291456 | tf_op jit(solution)/shard_map/rfn,ng->rgf/dot_general | solution.py:58
  31.1 6.1 %fusion = f32[32,512,32]{1,0,2:T(8,128)} fusion(f32[512,32,64]{0,1,2:T(8,128)S(1)} %get-tuple-element.6), kind=kOutput, calls=%fused_computation.3 | convolution fusion | flops 402681856 | bytes 6291456 | tf_op jit(solution)/shard_map/rfn,ng->rgf/dot_general | solution.py:63
  37.2 4.8 %multiply_bitcast_fusion.1 = f32[512,32,32]{0,1,2:T(8,128)S(1)} fusion(f32[32,512,32]{1,0,2:T(8,128)S(1)} %fusion.2, f32[512,32,64]{0,1,2:T(8,128)S(1)} %get-tuple-element.5), kind=kOutput, calls=%fused_computation.12 | convolution fusion | flops 403730432 | bytes 8388608 | tf_op jit(solution)/shard_map/rfn,ng->rgf/dot_general | solution.py:56
  43.2 4.8 %mul.263 = f32[2,8,32,4,1,256]{2,1,0,5,3,4:T(8,128)} reshape(f32[512,32,32]{0,2,1:T(8,128)S(1)} %copy.72) | data formatting | bytes 4194304 | tf_op jit(solution)/shard_map/mul | solution.py:67
  48.1 7.5 %multiply_bitcast_fusion = f32[512,32,32]{0,1,2:T(8,128)S(1)} fusion(f32[32,512,32]{1,0,2:T(8,128)} %fusion, f32[512,32,64]{0,1,2:T(8,128)} %copy-done.1), kind=kOutput, calls=%fused_computation.11 | convolution fusion | flops 403732480 | bytes 8388608 | tf_op jit(solution)/shard_map/rfn,ng->rgf/dot_general | solution.py:61
  56.8 4.4 %mul.266 = f32[2,8,32,4,1,256]{2,1,0,5,3,4:T(8,128)} reshape(f32[512,32,32]{0,2,1:T(8,128)S(1)} %copy.75) | data formatting | bytes 4194304 | tf_op jit(solution)/shard_map/mul | solution.py:68
  61.2 11.3 %pad_maximum_fusion = f32[2,8,32,4,2,256]{2,1,0,5,3,4:T(8,128)} fusion(f32[2,8,32,4,1,256]{2,1,0,5,3,4:T(8,128)} %mul.266, f32[2,8,32,4,1,256]{2,1,0,5,3,4:T(8,128)} %mul.263), kind=kLoop, calls=%fused_computation | loop fusion | flops 1048576 | bytes 8388608 | tf_op jit(solution)/shard_map/concatenate | solution.py:83
  72.5 15.2 %copy.76 = f32[2,8,32,4,2,256]{5,4,2,3,1,0:T(2,128)} copy(f32[2,8,32,4,2,256]{2,1,0,5,3,4:T(8,128)} %pad_maximum_fusion) | data formatting | bytes 8388608 | tf_op jit(solution)/shard_map/concatenate | solution.py:83
  87.7 6.5 %reshape.82 = f32[2,8,32,4,512]{4,2,3,1,0:T(8,128)} reshape(f32[2,8,32,4,2,256]{5,4,2,3,1,0:T(2,128)} %copy.76) | data formatting | bytes 8388608 | tf_op jit(solution)/shard_map/reshape | solution.py:83
  94.2 2.7 copy.77
  97.7 102.0 %all_to_all.33 = f32[2,32,32,512]{3,2,0,1:T(8,128)S(1)} all-to-all(f32[2,32,32,512]{3,2,0,1:T(8,128)S(1)} %copy.78), channel_id=1, replica_groups=mesh['freq'=4,'trace'=8] {'freq','trace'}, dimensions={1} | all-to-all | bytes 8388608 | tf_op jit(solution)/shard_map/all_to_all | solution.py:88
  199.7 7.1 %convolution_bitcast_fusion.2 = f32[512,512]{0,1:T(8,128)S(1)} fusion(f32[2048,512]{1,0:T(8,128)S(1)} %bitcast.84, f32[2048,512]{1,0:T(8,128)S(1)} %bitcast.85), kind=kOutput, calls=%fused_computation.18 | convolution fusion | flops 6442450944 | bytes 9437184 | tf_op jit(solution)/shard_map/xk,xc->kc/dot_general | solution.py:91
  207.2 1.7 collective-permute-done
  211.1 14.0 %collective-permute-done.1 = f32[256,512]{0,1:T(8,128)S(1)} collective-permute-done((f32[256,512]{0,1:T(8,128)S(1)}, f32[256,512]{0,1:T(8,128)S(1)}, u32[]{:S(2)}, u32[]{:S(2)}) %collective-permute-start.1) | collective-permute-done | bytes 524320 | tf_op jit(solution)/shard_map/ppermute | solution.py:22
  227.3 25.2 %collective-permute-done.2 = f32[256,512]{0,1:T(8,128)S(1)} collective-permute-done((f32[256,512]{0,1:T(8,128)S(1)}, f32[256,512]{0,1:T(8,128)S(1)}, u32[]{:S(2)}, u32[]{:S(2)}) %collective-permute-start.2) | collective-permute-done | bytes 524320 | tf_op jit(solution)/shard_map/ppermute | solution.py:22
  257.3 1.3 copy.79
  258.6 3.5 %all-to-all-start.1 = ((f32[512,2,256]{2,1,0:T(2,128)}), f32[512,2,256]{2,1,0:T(2,128)S(1)}, u32[]{:S(2)}, u32[]{:S(2)}) async-start(f32[512,2,256]{2,1,0:T(2,128)} %copy.79), calls=%async_computation.1 | async-start | bytes 2097152 | tf_op jit(solution)/shard_map/all_to_all | solution.py:117
  262.1 14.1 %all-to-all-done.1 = f32[512,2,256]{2,1,0:T(2,128)S(1)} async-done(((f32[512,2,256]{2,1,0:T(2,128)}), f32[512,2,256]{2,1,0:T(2,128)S(1)}, u32[]{:S(2)}, u32[]{:S(2)}) %all-to-all-start.1) | async-done | bytes 1048608 | tf_op jit(solution)/shard_map/all_to_all | solution.py:117
  276.6 4.8 %fusion.17 = f32[128,256]{1,0:T(8,128)S(1)} fusion(f32[128,2,1024]{0,2,1:T(8,128)S(1)} %bitcast.87, s32[256]{0:T(256)S(1)} %iota_multiply_fusion), kind=kOutput, calls=%fused_computation.35 | convolution fusion | flops 406323200 | bytes 656384 | tf_op jit(solution)/shard_map/dot_general | solution.py:26
  281.4 5.5 %fusion.12 = f32[128,256]{1,0:T(8,128)} fusion(f32[128,256]{1,0:T(8,128)S(1)} %fusion.17, f32[128,2,1024]{0,2,1:T(8,128)S(1)} %bitcast.88, s32[256]{0:T(256)S(1)} %iota_multiply_fusion), kind=kOutput, calls=%fused_computation.26 | convolution fusion | flops 406388736 | bytes 787456 | tf_op jit(solution)/shard_map/dot_general | solution.py:26
  (38 shorter events, 13.3 us)
Async XLA Ops:
  15.7 5.9 %copy-start = (f32[512,32,64]{0,1,2:T(8,128)S(1)}, f32[512,32,64]{0,1,2:T(8,128)}, u32[]{:S(2)}) copy-start(f32[512,32,64]{0,1,2:T(8,128)} %copy.68) | copy-start | bytes 12582916
  26.5 10.7 %copy-start.1 = (f32[512,32,64]{0,1,2:T(8,128)}, f32[512,32,64]{0,1,2:T(8,128)S(1)}, u32[]{:S(2)}) copy-start(f32[512,32,64]{0,1,2:T(8,128)S(1)} %get-tuple-element.5) | copy-start | bytes 12582916
  97.6 102.0 %copy-start.2 = (f32[64,32,512]{2,1,0:T(8,128)S(1)}, f32[64,32,512]{2,1,0:T(8,128)}, u32[]{:S(2)}) copy-start(f32[64,32,512]{2,1,0:T(8,128)} %param.5) | copy-start | bytes 12582916
  199.7 7.3 %copy-start.3 = (f32[3,256,1024]{2,1,0:T(8,128)S(1)}, f32[3,256,1024]{2,1,0:T(8,128)}, u32[]{:S(2)}) copy-start(f32[3,256,1024]{2,1,0:T(8,128)} %param.6) | copy-start | bytes 9437188
  206.9 2.0 collective-permute-start
  211.0 14.0 %collective-permute-start.1 = (f32[256,512]{0,1:T(8,128)S(1)}, f32[256,512]{0,1:T(8,128)S(1)}, u32[]{:S(2)}, u32[]{:S(2)}) collective-permute-start(f32[256,512]{0,1:T(8,128)S(1)} %pad_maximum_fusion.12), channel_id=1, source_target_pairs={{0,2},{2,0},{1,3},{3,1},{4,6},{6,4},{5,7},{7,5},{8,10},{10,8},{9,1... | collective-permute-start | bytes 1572872 | tf_op jit(solution)/shard_map/ppermute | solution.py:22
  227.1 27.8 %copy-start.4 = (f32[512,512]{1,0:T(8,128)S(1)}, f32[512,512]{1,0:T(8,128)}, u32[]{:S(2)}) copy-start(f32[512,512]{1,0:T(8,128)} %param.7) | copy-start | bytes 3145732
  227.2 25.3 %collective-permute-start.2 = (f32[256,512]{0,1:T(8,128)S(1)}, f32[256,512]{0,1:T(8,128)S(1)}, u32[]{:S(2)}, u32[]{:S(2)}) collective-permute-start(f32[256,512]{0,1:T(8,128)S(1)} %pad_maximum_fusion.13), channel_id=1, source_target_pairs={{0,4},{4,0},{1,5},{5,1},{2,6},{6,2},{3,7},{7,3},{8,12},{12,8},{9,1... | collective-permute-start | bytes 1572872 | tf_op jit(solution)/shard_map/ppermute | solution.py:22
  258.6 17.6 %all-to-all-start.1 = ((f32[512,2,256]{2,1,0:T(2,128)}), f32[512,2,256]{2,1,0:T(2,128)S(1)}, u32[]{:S(2)}, u32[]{:S(2)}) async-start(f32[512,2,256]{2,1,0:T(2,128)} %copy.79), calls=%async_computation.1 | async-start | bytes 2097152 | tf_op jit(solution)/shard_map/all_to_all | solution.py:117
where the time goes:
time: 291 us; the launch traced here: 287 us
  blocking collectives  102 us (35%)
  matrix products  59.4 us (20%)
  waiting for transfers between devices  54.9 us (19%)
  local copies, waits for them, and re-layouts  54.3 us (19%)
  other arithmetic  12.1 us (4%)
  starting transfers between devices  3.73 us (1%)
    all_to_all x1, blocking collectives, body(): lax.all_to_all(spectrum, ('freq', 'trace'), split_axis=1, concat_axis=0,...  102 us
    ppermute x3, waiting for transfers between devices, from_partner(): return lax.ppermute(block, axis, route)  40.8 us
    dot_general x10, matrix products, product(): jnp.dot(left, right, precision=EXACT, preferred_element_type=jnp.float32)  18.6 us
    another operation x2, local copies, waits for them, and re-layouts, time_spectrum(): blocks = samples.reshape(row_count, outer, inner)  15.6 us
    concatenate x1, local copies, waits for them, and re-layouts, body(): jnp.concatenate([spec_real, spec_imag], axis=4)  15.2 us
    all_to_all x1, waiting for transfers between devices, body(): lax.all_to_all(image_both, 'freq', split_axis=0, concat_axis=2, tiled=True)  14.1 us
    concatenate x1, other arithmetic, body(): jnp.concatenate([spec_real, spec_imag], axis=4)  11.3 us
    dot_general x1, matrix products, time_spectrum(): jnp.einsum('rfn,ng->rgf', turned_real, second_sin, precision=EXACT, prefe...  7.47 us
  transfers between devices with their start and end apart: 4, of which 4 were waited for; matrix products, arithmetic and copies ran while one was open for 0% of the time, Pallas kernels for 0%

commit v1 on v0

v1 whole, which is shorter than its diff:
```python
import math

import jax
import jax.numpy as jnp
import numpy as np
from jax import lax
from jax.sharding import PartitionSpec as P

FREQS = 1024
TAUS = 256


SPLIT = lax.Precision.HIGH


def from_partner(block, axis, apart):
    count = lax.axis_size(axis)
    route = []
    for low in range(count):
        high = low | 1 << apart
        if high != low and high < count:
            route += [(low, high), (high, low)]
    return lax.ppermute(block, axis, route)


def product(left, right):
    return jnp.dot(left, right, precision=SPLIT, preferred_element_type=jnp.float32)


def lag_series(sample_count):
    lags = np.arange(sample_count)
    turns = (np.arange(FREQS)[:, None] * lags[None, :]) % sample_count
    return np.exp(2j * np.pi * turns / sample_count).sum(axis=0)


def imag_table(sample_count):
    series = lag_series(sample_count).imag
    step = sample_count // (4 * TAUS)
    lags = (np.arange(TAUS)[None, :] * step - np.arange(sample_count)[:, None]) % sample_count
    return (series[lags] / math.sqrt(sample_count * FREQS)).astype(np.float32)


def body(traces, source_weights, level_weights, slowness_weights):
    freq_count = lax.axis_size("freq")
    trace_count = lax.axis_size("trace")
    shot_dev, offset_count, sample_count = traces.shape
    tau_dev = TAUS // freq_count
    box_offsets = offset_count // trace_count
    coeff_count = source_weights.shape[2] // 2
    step = sample_count // (4 * TAUS)
    norm = 1.0 / math.sqrt(sample_count * FREQS)
    samples = traces.reshape(-1, sample_count)
    odd = (jnp.arange(sample_count) % 2 == 1).astype(jnp.float32)
    odd_sum = jnp.sum(samples * odd, axis=1, keepdims=True) * norm
    span = TAUS * step
    pick = (jnp.arange(span)[:, None] == jnp.arange(TAUS)[None, :] * step).astype(jnp.float32)
    folded_real = product(samples[:, :span], pick) * (FREQS * norm) + odd_sum
    folded_imag = product(samples, jnp.asarray(imag_table(sample_count)))
    folded_real = folded_real.reshape(shot_dev, trace_count, box_offsets, freq_count, 1, tau_dev)
    folded_imag = folded_imag.reshape(shot_dev, trace_count, box_offsets, freq_count, 1, tau_dev)
    folded = jnp.concatenate([folded_real, folded_imag], axis=4).reshape(
        shot_dev, trace_count, box_offsets, freq_count, 2 * tau_dev
    )
    folded = jnp.transpose(folded, (3, 1, 0, 2, 4)).reshape(
        freq_count * trace_count, shot_dev * box_offsets, 2 * tau_dev
    )
    folded = lax.all_to_all(folded, ("freq", "trace"), split_axis=0, concat_axis=0, tiled=True)
    folded = folded.reshape(-1, 2 * tau_dev)
    sources = source_weights.reshape(-1, 2 * coeff_count)
    gram = jnp.einsum(
        "xk,xc->kc", sources, folded, precision=SPLIT, preferred_element_type=jnp.float32
    )
    coeff_real = gram[:coeff_count, :tau_dev] - gram[coeff_count:, tau_dev:]
    coeff_imag = gram[:coeff_count, tau_dev:] + gram[coeff_count:, :tau_dev]
    coeffs = jnp.concatenate([coeff_real, coeff_imag], axis=1)
    for level_no in range(level_weights.shape[0]):
        partner = from_partner(coeffs, "trace", level_no)
        weights = level_weights[level_no]
        stacked = jnp.concatenate([coeffs, partner], axis=0)
        real_rows = product(weights[:, : 2 * coeff_count], stacked)
        imag_rows = product(weights[:, 2 * coeff_count :], stacked)
        coeffs = jnp.concatenate(
            [
                real_rows[:, :tau_dev] - imag_rows[:, tau_dev:],
                real_rows[:, tau_dev:] + imag_rows[:, :tau_dev],
            ],
            axis=1,
        )
    image = product(slowness_weights[:, :coeff_count], coeffs[:, :tau_dev]) - product(
        slowness_weights[:, coeff_count:], coeffs[:, tau_dev:]
    )
    return lax.all_to_all(image, "freq", split_axis=0, concat_axis=1, tiled=True)


def solution(mesh):
    return jax.shard_map(
        body,
        mesh=mesh,
        in_specs=(
            P(("freq", "trace"), None, None),
            P(None, "trace", None),
            P(None, "trace", None),
            P("trace", None),
        ),
        out_specs=P(("trace", "freq"), None),
        check_vma=False,
    )
```

time: 291 us -> 77.6 us (0.27); the launches traced: 287 us -> 77.4 us
  blocking collectives: 102 us -> 42 us
  local copies, waits for them, and re-layouts: 54.3 us -> 5.08 us
  matrix products: 59.4 us -> 12.1 us
  waiting for transfers between devices: 54.9 us -> 14.8 us
  other arithmetic: 12.1 us -> 2.88 us
  starting transfers between devices: 3.73 us -> 0.21 us
    all_to_all x1 -> x2, blocking collectives: 102 us -> 42 us  [the longest x1 34.6 us: body(): lax.all_to_all(folded, ('freq', 'trace'), split_axis=0, concat_axis=0, ti...]
    dot_general x17 -> x11, matrix products: 59.4 us -> 12.1 us  [the longest x10 10.6 us: product(): jnp.dot(left, right, precision=SPLIT, preferred_element_type=jnp.float32)]
    ppermute x3, waiting for transfers between devices: 40.8 us -> 14.8 us  [from_partner(): return lax.ppermute(block, axis, route)]
    another operation x3 -> x0, local copies, waits for them, and re-layouts: 16.9 us -> none  [the longest x2 15.6 us: time_spectrum(): blocks = samples.reshape(row_count, outer, inner)]
    all_to_all x1 -> x0, waiting for transfers between devices: 14.1 us -> none  [body(): lax.all_to_all(image_both, 'freq', split_axis=0, concat_axis=2, tiled=True)]
    concatenate x1, local copies, waits for them, and re-layouts: 15.2 us -> 1.91 us  [body(): jnp.concatenate([folded_real, folded_imag], axis=4)]
    mul x4 -> x0, local copies, waits for them, and re-layouts: 11.7 us -> none  [the longest x2 6.03 us: time_spectrum(): final_real = final_real.reshape(row_count, upper * outer) * scaled]
    concatenate x3, other arithmetic: 11.4 us -> 0.25 us  [the longest x1 0.22 us: body(): jnp.concatenate([folded_real, folded_imag], axis=4)]
  transfers between devices with their start and end apart: 4 -> 3, of which waited for: 4 -> 3; matrix products, arithmetic and copies ran while one was open for 0% -> 1% of each run, Pallas kernels for 0% -> 0%
where the time goes in v1:
time: 77.6 us; the launch traced here: 77.4 us
  blocking collectives  42 us (54%)
  waiting for transfers between devices  14.8 us (19%)
  matrix products  12.1 us (16%)
  local copies, waits for them, and re-layouts  5.08 us (7%)
  other arithmetic  2.88 us (4%)
    all_to_all x1, blocking collectives, body(): lax.all_to_all(folded, ('freq', 'trace'), split_axis=0, concat_axis=0, ti...  34.6 us
    ppermute x3, waiting for transfers between devices, from_partner(): return lax.ppermute(block, axis, route)  14.8 us
    dot_general x10, matrix products, product(): jnp.dot(left, right, precision=SPLIT, preferred_element_type=jnp.float32)  10.6 us
    all_to_all x1, blocking collectives, body(): lax.all_to_all(image, 'freq', split_axis=0, concat_axis=1, tiled=True)  7.41 us
    reduce_sum x1, other arithmetic, body(): odd_sum = jnp.sum(samples * odd, axis=1, keepdims=True) * norm  2.55 us
    concatenate x1, local copies, waits for them, and re-layouts, body(): jnp.concatenate([folded_real, folded_imag], axis=4)  1.91 us
  transfers between devices with their start and end apart: 3, of which 3 were waited for; matrix products, arithmetic and copies ran while one was open for 1% of the time, Pallas kernels for 0%

profile of v1, /device:TPU:0, one launch (start us, length us, event | category | flops | bytes accessed | tf_op | source)
XLA Modules:
  0.0 77.4 jit_solution(5626983923797784)
XLA Ops:
  0.0 2.6 %multiply_reduce_fusion = f32[2,256]{1,0:T(2,128)S(1)} fusion(f32[2,256,2048]{2,1,0:T(8,128)} %param.5, f32[2048]{0:T(1024)S(1)} %fusion.22), kind=kLoop, calls=%fused_computation | loop fusion | flops 2096640 | bytes 4204544 | tf_op jit(solution)/shard_map/reduce_sum | solution.py:54
  2.6 1.8 %fusion.1 = f32[512,256]{0,1:T(8,128)S(1)} fusion(f32[512,2048]{1,0:T(8,128)} %bitcast.55, f32[512]{0:T(512)S(1)} %bitcast.63, s32[256]{0:T(256)S(1)} %iota_multiply_fusion), kind=kOutput, calls=%fused_computation.5 | convolution fusion | flops 403177472 | bytes 1575936 | tf_op jit(solution)/shard_map/dot_general | solution.py:27
  4.4 0.2 copy.8
  4.6 0.5 reshape.62
  5.2 5.6 %convolution_bitcast_fusion = f32[2,8,32,4,1,64]{5,2,1,0,3,4:T(8,128)S(1)} fusion(f32[4,64,2048,1,1]{2,1,4,3,0:T(8,128)} %constant.30, f32[2,8,32,2048,1]{3,2,1,0,4:T(8,128)} %bitcast.56), kind=kOutput, calls=%fused_computation.2 | convolution fusion | flops 1610612736 | bytes 6815744 | tf_op jit(solution)/shard_map/dot_general | solution.py:27
  10.8 0.2 pad_maximum_fusion
  11.0 1.9 %copy.10 = f32[2,8,32,4,2,64]{5,4,2,3,1,0:T(2,128)S(1)} copy(f32[2,8,32,4,2,64]{5,2,1,0,3,4:T(8,128)S(1)} %pad_maximum_fusion) | data formatting | bytes 2097152 | tf_op jit(solution)/shard_map/concatenate | solution.py:61
  12.9 1.1 %reshape.64 = f32[2,8,32,4,128]{4,2,3,1,0:T(8,128)S(1)} reshape(f32[2,8,32,4,2,64]{5,4,2,3,1,0:T(2,128)S(1)} %copy.10) | data formatting | bytes 2097152 | tf_op jit(solution)/shard_map/reshape | solution.py:61
  14.2 34.6 %all_to_all.24 = f32[32,64,128]{2,1,0:T(8,128)S(1)} all-to-all(f32[32,64,128]{2,1,0:T(8,128)S(1)} %bitcast.59), channel_id=1, replica_groups=mesh['freq'=4,'trace'=8] {'freq','trace'}, dimensions={0} | all-to-all | bytes 2097152 | tf_op jit(solution)/shard_map/all_to_all | solution.py:67
  48.8 1.5 %convolution_bitcast_fusion.1 = f32[512,128]{0,1:T(8,128)S(1)} fusion(f32[2048,128]{1,0:T(8,128)S(1)} %bitcast.60, f32[2048,512]{1,0:T(8,128)S(1)} %bitcast.58), kind=kOutput, calls=%fused_computation.6 | convolution fusion | flops 805306368 | bytes 5505024 | tf_op jit(solution)/shard_map/xk,xc->kc/dot_general | solution.py:70
  50.5 0.4 slice_bitcast_fusion.2
  50.9 0.9 %collective-permute-done = f32[256,128]{0,1:T(8,128)S(1)} collective-permute-done((f32[256,128]{0,1:T(8,128)S(1)}, f32[256,128]{0,1:T(8,128)S(1)}, u32[]{:S(2)}, u32[]{:S(2)}) %collective-permute-start) | collective-permute-done | bytes 131104 | tf_op jit(solution)/shard_map/ppermute | solution.py:23
  51.8 0.4 convolution_bitcast_fusion.6
  52.2 0.4 convolution_bitcast_fusion.7
  52.7 5.5 %collective-permute-done.1 = f32[256,128]{0,1:T(8,128)S(1)} collective-permute-done((f32[256,128]{0,1:T(8,128)S(1)}, f32[256,128]{0,1:T(8,128)S(1)}, u32[]{:S(2)}, u32[]{:S(2)}) %collective-permute-start.1) | collective-permute-done | bytes 131104 | tf_op jit(solution)/shard_map/ppermute | solution.py:23
  58.3 0.4 convolution_bitcast_fusion.4
  58.7 0.4 convolution_bitcast_fusion.5
  59.2 8.4 %collective-permute-done.2 = f32[256,128]{0,1:T(8,128)S(1)} collective-permute-done((f32[256,128]{0,1:T(8,128)S(1)}, f32[256,128]{0,1:T(8,128)S(1)}, u32[]{:S(2)}, u32[]{:S(2)}) %collective-permute-start.2) | collective-permute-done | bytes 131104 | tf_op jit(solution)/shard_map/ppermute | solution.py:23
  67.6 0.4 convolution_bitcast_fusion.2
  68.0 0.4 convolution_bitcast_fusion.3
  68.5 0.4 fusion.11
  68.9 0.4 fusion.2
  69.3 7.4 %all_to_all.25 = f32[4,128,64]{1,2,0:T(8,128)S(1)} all-to-all(f32[4,128,64]{1,2,0:T(8,128)S(1)} %bitcast.61), channel_id=1, replica_groups=mesh['freq'=4,'trace'=8] {'freq'}, dimensions={0} | all-to-all | bytes 262144 | tf_op jit(solution)/shard_map/all_to_all | solution.py:92
  76.7 0.8 copy.13
  (22 shorter events, 0.5 us)
Async XLA Ops:
  14.1 34.7 %copy-start = (f32[64,32,512]{2,1,0:T(8,128)S(1)}, f32[64,32,512]{2,1,0:T(8,128)}, u32[]{:S(2)}) copy-start(f32[64,32,512]{2,1,0:T(8,128)} %param.6) | copy-start | bytes 12582916
  14.2 36.3 %copy-start.1 = (f32[3,256,1024]{2,1,0:T(8,128)S(1)}, f32[3,256,1024]{2,1,0:T(8,128)}, u32[]{:S(2)}) copy-start(f32[3,256,1024]{2,1,0:T(8,128)} %param.7) | copy-start | bytes 9437188
  50.4 1.4 %collective-permute-start = (f32[256,128]{0,1:T(8,128)S(1)}, f32[256,128]{0,1:T(8,128)S(1)}, u32[]{:S(2)}, u32[]{:S(2)}) collective-permute-start(f32[256,128]{0,1:T(8,128)S(1)} %pad_maximum_fusion.10), channel_id=1, source_target_pairs={{0,1},{1,0},{2,3},{3,2},{4,5},{5,4},{6,7},{7,6},{8,9},{9,8},{10,11... | collective-permute-start | bytes 393224 | tf_op jit(solution)/shard_map/ppermute | solution.py:23
  50.9 17.6 %copy-start.2 = (f32[512,512]{1,0:T(8,128)S(1)}, f32[512,512]{1,0:T(8,128)}, u32[]{:S(2)}) copy-start(f32[512,512]{1,0:T(8,128)} %param.8) | copy-start | bytes 3145732
  52.7 5.6 %collective-permute-start.1 = (f32[256,128]{0,1:T(8,128)S(1)}, f32[256,128]{0,1:T(8,128)S(1)}, u32[]{:S(2)}, u32[]{:S(2)}) collective-permute-start(f32[256,128]{0,1:T(8,128)S(1)} %pad_maximum_fusion.11), channel_id=1, source_target_pairs={{0,2},{2,0},{1,3},{3,1},{4,6},{6,4},{5,7},{7,5},{8,10},{10,8},{9,1... | collective-permute-start | bytes 393224 | tf_op jit(solution)/shard_map/ppermute | solution.py:23
  59.2 8.5 %collective-permute-start.2 = (f32[256,128]{0,1:T(8,128)S(1)}, f32[256,128]{0,1:T(8,128)S(1)}, u32[]{:S(2)}, u32[]{:S(2)}) collective-permute-start(f32[256,128]{0,1:T(8,128)S(1)} %pad_maximum_fusion.12), channel_id=1, source_target_pairs={{0,4},{4,0},{1,5},{5,1},{2,6},{6,2},{3,7},{7,3},{8,12},{12,8},{9,1... | collective-permute-start | bytes 393224 | tf_op jit(solution)/shard_map/ppermute | solution.py:23

commit v2 on v1

--- a/solution.py
+++ b/solution.py
@@ -1,9 +1,12 @@
+import functools
 import math
 
 import jax
 import jax.numpy as jnp
 import numpy as np
 from jax import lax
+from jax.experimental import pallas as pl
+from jax.experimental.pallas import tpu as pltpu
 from jax.sharding import PartitionSpec as P
 
 FREQS = 1024
@@ -92,9 +95,354 @@
     return lax.all_to_all(image, "freq", split_axis=0, concat_axis=1, tiled=True)
 
 
+MESH = pl.DeviceIdType.MESH
+CORES = 2
+
+
+def halves(value):
+    high = value.astype(jnp.bfloat16)
+    low = (value - high.astype(jnp.float32)).astype(jnp.bfloat16)
+    return high, low
+
+
+def dot(left, right):
+    return jnp.dot(left, right, preferred_element_type=jnp.float32)
+
+
+def dot_pairs(left, right):
+    return dot(left[0], right[0]) + (dot(left[0], right[1]) + dot(left[1], right[0]))
+
+
+def exclusive_or(left, right, count):
+    total, bit = 0, 1
+    while bit < count:
+        total = total + (left // bit + right // bit) % 2 * bit
+        bit *= 2
+    return total
+
+
+def turned(real_rows, imag_rows, tau_dev):
+    swapped = jnp.concatenate([-imag_rows[:, tau_dev:], imag_rows[:, :tau_dev]], axis=1)
+    return real_rows + swapped
+
+
+def kernel(
+    freq_count, trace_count,
+    x_hbm, s_hbm, w_hbm, e_hbm, table_hi_hbm, table_lo_hbm,
+    out_ref,
+    x_ref, s_ref, w_ref, e_ref, table_hi, table_lo,
+    st_hi, st_lo, w_hi, w_lo, e_hi, e_lo,
+    send, recv, acc, level_send, level_recv, image_send, image_recv,
+    x_sems, load_sems, send_sems, recv_sems, level_ss, level_rs, image_ss, image_rs,
+):
+    fi, ti = lax.axis_index("freq"), lax.axis_index("trace")
+    devices = freq_count * trace_count
+    planes = trace_count // CORES
+    me = fi * trace_count + ti
+    my_plane, my_core = ti // CORES, ti % CORES
+    shot_dev, offset_count, sample_count = x_ref.shape
+    box_offsets = offset_count // trace_count
+    coeff_count = w_ref.shape[1]
+    tau_dev = TAUS // freq_count
+    step = sample_count // (4 * TAUS)
+    norm = 1.0 / math.sqrt(sample_count * FREQS)
+    span = TAUS * step
+    plane_offsets = CORES * box_offsets
+
+    barrier = pltpu.get_barrier_semaphore()
+
+    def greet(i, _):
+        other = (me + i) % devices
+        pl.semaphore_signal(
+            barrier,
+            inc=1,
+            device_id={"freq": other // trace_count, "trace": other % trace_count},
+            device_id_type=MESH,
+        )
+        return 0
+
+    lax.fori_loop(1, devices, greet, 0)
+
+    def plane_at(turn):
+        return exclusive_or(my_plane, planes - 1 - turn, planes)
+
+    def load_x(turn):
+        rows = pl.ds(pl.multiple_of(plane_at(turn) * plane_offsets, plane_offsets), plane_offsets)
+        return pltpu.make_async_copy(x_hbm.at[:, rows, :], x_ref.at[:, rows, :], x_sems.at[turn])
+
+    loads = [
+        pltpu.make_async_copy(source, target, load_sems.at[i])
+        for i, (source, target) in enumerate(
+            [
+                (table_hi_hbm, table_hi),
+                (table_lo_hbm, table_lo),
+                (s_hbm, s_ref),
+                (w_hbm, w_ref),
+                (e_hbm, e_ref),
+            ]
+        )
+    ]
+    loads[0].start()
+    load_x(0).start()
+    loads[1].start()
+    for turn in range(1, planes):
+        load_x(turn).start()
+    for load in loads[2:]:
+        load.start()
+
+    pick = (
+        lax.broadcasted_iota(jnp.int32, (span, TAUS), 0)
+        == lax.broadcasted_iota(jnp.int32, (span, TAUS), 1) * step
+    ).astype(jnp.bfloat16)
+    odd = lax.broadcasted_iota(jnp.int32, (1, sample_count), 1) % 2 == 1
+    loads[0].wait()
+    loads[1].wait()
+
+    def block_copy(plane, f, core):
+        return pltpu.make_async_remote_copy(
+            src_ref=send.at[plane, f, core],
+            dst_ref=recv.at[my_plane, fi, my_core],
+            send_sem=send_sems.at[plane, f, core],
+            recv_sem=recv_sems.at[my_plane, fi, my_core],
+            device_id={"freq": f, "trace": plane * CORES + core},
+            device_id_type=MESH,
+        )
+
+    def arrival(plane, f, core):
+        return pltpu.make_async_remote_copy(
+            src_ref=send.at[plane, f, core],
+            dst_ref=recv.at[plane, f, core],
+            send_sem=send_sems.at[plane, f, core],
+            recv_sem=recv_sems.at[plane, f, core],
+            device_id={"freq": f, "trace": plane * CORES + core},
+            device_id_type=MESH,
+        )
+
+    def is_me(plane, f, core):
+        return (f * trace_count + plane * CORES + core) == me
+
+    def fold(turn, _):
+        plane = plane_at(turn)
+        load_x(turn).wait()
+        rows = pl.ds(pl.multiple_of(plane * plane_offsets, plane_offsets), plane_offsets)
+        samples = x_ref[:, rows, :].reshape(shot_dev * plane_offsets, sample_count)
+        high, low = halves(samples)
+        odd_sum = jnp.sum(jnp.where(odd, samples, 0.0), axis=1, keepdims=True) * norm
+        imag = dot_pairs((high, low), (table_hi[...], table_lo[...]))
+        real = (dot(high[:, :span], pick) + dot(low[:, :span], pick)) * (FREQS * norm) + odd_sum
+        for f in range(freq_count):
+            columns = slice(f * tau_dev, (f + 1) * tau_dev)
+            block = jnp.concatenate([real[:, columns], imag[:, columns]], axis=1)
+            block = block.reshape(shot_dev, CORES, box_offsets, 2 * tau_dev)
+            for core in range(CORES):
+                send[plane, f, core] = block[:, core]
+
+        @pl.when(turn == 0)
+        def _():
+            pl.semaphore_wait(barrier, devices - 1)
+
+        def start(i, _):
+            f, core = (fi + i // CORES) % freq_count, i % CORES
+
+            @pl.when(jnp.logical_not(is_me(plane, f, core)))
+            def _():
+                block_copy(plane, f, core).start()
+
+            return 0
+
+        lax.fori_loop(0, freq_count * CORES, start, 0)
+        return 0
+
+    lax.fori_loop(0, planes, fold, 0)
+    recv[my_plane, fi, my_core] = send[my_plane, fi, my_core]
+
+    loads[2].wait()
+    pair_shots = CORES * shot_dev
+    pair_rows = pair_shots * box_offsets
+
+    def turn_sources(i, _):
+        f, plane = i // planes, i % planes
+        part = s_ref[pl.ds(i * pair_shots, pair_shots)].reshape(pair_rows, 2 * coeff_count)
+        high, low = halves(part.T)
+        columns = pl.ds(pl.multiple_of(f * pair_rows, pair_rows), pair_rows)
+        st_hi[plane, :, columns] = high
+        st_lo[plane, :, columns] = low
+        return 0
+
+    lax.fori_loop(0, freq_count * planes, turn_sources, 0)
+    loads[3].wait()
+
+    def split_level(level, _):
+        w_hi[level], w_lo[level] = halves(w_ref[level])
+        return 0
+
+    lax.fori_loop(0, w_ref.shape[0], split_level, 0)
+    loads[4].wait()
+    e_hi[...], e_lo[...] = halves(e_ref[...])
+
+    acc[...] = jnp.zeros_like(acc)
+
+    def gram(turn, _):
+        plane = exclusive_or(my_plane, turn, planes)
+
+        def wait_for(i, _):
+            f, core = i // CORES, i % CORES
+
+            @pl.when(jnp.logical_not(is_me(plane, f, core)))
+            def _():
+                arrival(plane, f, core).wait_recv()
+
+            return 0
+
+        lax.fori_loop(0, freq_count * CORES, wait_for, 0)
+        blocks = recv[plane].reshape(freq_count * pair_rows, 2 * tau_dev)
+        acc[...] += dot_pairs((st_hi[plane], st_lo[plane]), halves(blocks))
+        return 0
+
+    lax.fori_loop(0, planes, gram, 0)
+    coeffs = turned(acc[:coeff_count], acc[coeff_count:], tau_dev)
+
+    for level in range(w_ref.shape[0]):
+        level_send[level] = coeffs
+        flip = 1 << level
+        partner = ti + (1 - 2 * (ti // flip % 2)) * flip
+        exchange = pltpu.make_async_remote_copy(
+            src_ref=level_send.at[level],
+            dst_ref=level_recv.at[level],
+            send_sem=level_ss.at[level],
+            recv_sem=level_rs.at[level],
+            device_id={"freq": fi, "trace": partner},
+            device_id_type=MESH,
+        )
+        exchange.start()
+
+        def part(block, pairs):
+            columns = slice(block * coeff_count, (block + 1) * coeff_count)
+            return dot_pairs((w_hi[level, :, columns], w_lo[level, :, columns]), pairs)
+
+        own = halves(coeffs)
+        real_rows, imag_rows = part(0, own), part(2, own)
+        exchange.wait()
+        other = halves(level_recv[level])
+        coeffs = turned(real_rows + part(1, other), imag_rows + part(3, other), tau_dev)
+
+    pairs = halves(coeffs)
+    image = (
+        dot_pairs((e_hi[:, :coeff_count], e_lo[:, :coeff_count]), pairs)[:, :tau_dev]
+        - dot_pairs((e_hi[:, coeff_count:], e_lo[:, coeff_count:]), pairs)[:, tau_dev:]
+    )
+    rows_out = out_ref.shape[0]
+    for f in range(freq_count):
+        image_send[f] = image[f * rows_out : (f + 1) * rows_out]
+
+    def image_copy(target, source):
+        return pltpu.make_async_remote_copy(
+            src_ref=image_send.at[target],
+            dst_ref=image_recv.at[source],
+            send_sem=image_ss.at[target],
+            recv_sem=image_rs.at[source],
+            device_id={"freq": target, "trace": ti},
+            device_id_type=MESH,
+        )
+
+    def start_image(i, _):
+        image_copy((fi + i) % freq_count, fi).start()
+        return 0
+
+    def wait_image(i, _):
+        other = (fi + i) % freq_count
+        image_copy(other, fi).wait_send()
+        image_copy(other, other).wait_recv()
+        return 0
+
+    lax.fori_loop(1, freq_count, start_image, 0)
+    image_recv[fi] = image_send[fi]
+
+    def wait_sent(i, _):
+        plane, f, core = i // (freq_count * CORES), i // CORES % freq_count, i % CORES
+
+        @pl.when(jnp.logical_not(is_me(plane, f, core)))
+        def _():
+            block_copy(plane, f, core).wait_send()
+
+        return 0
+
+    lax.fori_loop(0, devices, wait_sent, 0)
+    lax.fori_loop(1, freq_count, wait_image, 0)
+    out_ref[...] = jnp.concatenate([image_recv[f] for f in range(freq_count)], axis=1)
+
+
+def fused(traces, source_weights, level_weights, slowness_weights):
+    freq_count = lax.axis_size("freq")
+    trace_count = lax.axis_size("trace")
+    devices = freq_count * trace_count
+    planes = trace_count // CORES
+    shot_dev, offset_count, sample_count = traces.shape
+    box_offsets = offset_count // trace_count
+    columns = source_weights.shape[2]
+    coeff_count = columns // 2
+    levels = level_weights.shape[0]
+    slow_dev = slowness_weights.shape[0]
+    width = 2 * (TAUS // freq_count)
+    table = imag_table(sample_count)
+    table_hi = table.astype(jnp.bfloat16)
+    table_lo = (table - table_hi.astype(np.float32)).astype(jnp.bfloat16)
+    rows = freq_count * CORES * shot_dev * box_offsets
+    blocks = (planes, freq_count, CORES)
+    f32, bf16, dma = jnp.float32, jnp.bfloat16, pltpu.SemaphoreType.DMA
+    rows_out = slow_dev // freq_count
+    return pl.pallas_call(
+        functools.partial(kernel, freq_count, trace_count),
+        out_shape=jax.ShapeDtypeStruct((rows_out, TAUS), f32),
+        in_specs=[pl.BlockSpec(memory_space=pl.ANY)] * 6,
+        out_specs=pl.BlockSpec(memory_space=pltpu.VMEM),
+        scratch_shapes=[
+            pltpu.VMEM(traces.shape, f32),
+            pltpu.VMEM(source_weights.shape, f32),
+            pltpu.VMEM(level_weights.shape, f32),
+            pltpu.VMEM(slowness_weights.shape, f32),
+            pltpu.VMEM(table.shape, bf16),
+            pltpu.VMEM(table.shape, bf16),
+            pltpu.VMEM((planes, columns, rows), bf16),
+            pltpu.VMEM((planes, columns, rows), bf16),
+            pltpu.VMEM(level_weights.shape, bf16),
+            pltpu.VMEM(level_weights.shape, bf16),
+            pltpu.VMEM(slowness_weights.shape, bf16),
+            pltpu.VMEM(slowness_weights.shape, bf16),
+            pltpu.VMEM(blocks + (shot_dev, box_offsets, width), f32),
+            pltpu.VMEM(blocks + (shot_dev, box_offsets, width), f32),
+            pltpu.VMEM((columns, width), f32),
+            pltpu.VMEM((levels, coeff_count, width), f32),
+            pltpu.VMEM((levels, coeff_count, width), f32),
+            pltpu.VMEM((freq_count, rows_out, width // 2), f32),
+            pltpu.VMEM((freq_count, rows_out, width // 2), f32),
+            dma((planes,)),
+            dma((5,)),
+            dma(blocks),
+            dma(blocks),
+            dma((levels,)),
+            dma((levels,)),
+            dma((freq_count,)),
+            dma((freq_count,)),
+        ],
+        compiler_params=pltpu.CompilerParams(
+            collective_id=0, has_side_effects=True, vmem_limit_bytes=60 * 1024 * 1024
+        ),
+        name="fold_and_butterfly",
+    )(
+        traces,
+        source_weights,
+        level_weights,
+        slowness_weights,
+        jnp.asarray(table_hi),
+        jnp.asarray(table_lo),
+    )
+
+
 def solution(mesh):
+    lanes = 2 * TAUS // mesh.shape["freq"]
     return jax.shard_map(
-        body,
+        fused if lanes % 128 == 0 else body,
         mesh=mesh,
         in_specs=(
             P(("freq", "trace"), None, None),

time: 77.6 us -> 55.9 us (0.72)
  Pallas kernels: 0 us -> 54.2 us
  blocking collectives: 42 us -> 0 us
  waiting for transfers between devices: 14.8 us -> 0 us
  matrix products: 12.1 us -> 0 us
  local copies, waits for them, and re-layouts: 5.08 us -> 1.57 us
  other arithmetic: 2.88 us -> 0 us
    pallas_call x0 -> x1, Pallas kernels: none -> 54.2 us  [fused(): pl.pallas_call(functools.partial(kernel, freq_count, trace_count), out_sh...]
    all_to_all x2 -> x0, blocking collectives: 42 us -> none  [the longest x1 34.6 us: body(): lax.all_to_all(folded, ('freq', 'trace'), split_axis=0, concat_axis=0, ti...]
    ppermute x3 -> x0, waiting for transfers between devices: 14.8 us -> none  [from_partner(): return lax.ppermute(block, axis, route)]
    dot_general x11 -> x0, matrix products: 12.1 us -> none  [the longest x10 10.6 us: product(): jnp.dot(left, right, precision=SPLIT, preferred_element_type=jnp.float32)]
    reduce_sum x1 -> x0, other arithmetic: 2.55 us -> none  [body(): odd_sum = jnp.sum(samples * odd, axis=1, keepdims=True) * norm]
    concatenate x1 -> x0, local copies, waits for them, and re-layouts: 1.91 us -> none  [body(): jnp.concatenate([folded_real, folded_imag], axis=4)]
    reshape x3 -> x0, local copies, waits for them, and re-layouts: 1.71 us -> none  [the longest x1 1.13 us: body(): jnp.concatenate([folded_real, folded_imag], axis=4)]
    unnamed x7 -> x1, local copies, waits for them, and re-layouts: 0.02 us -> 1.57 us
  transfers between devices with their start and end apart: 3 -> 0, of which waited for: 3 -> 0; matrix products, arithmetic and copies ran while one was open for 1% -> 0% of each run, Pallas kernels for 0% -> 0%
where the time goes in v2:
time: 55.9 us; the launch traced here: 55.8 us
  Pallas kernels  54.2 us (97%)
  local copies, waits for them, and re-layouts  1.57 us (3%)
    pallas_call x1, Pallas kernels, fused(): pl.pallas_call(functools.partial(kernel, freq_count, trace_count), out_sh...  54.2 us
    unnamed x1, local copies, waits for them, and re-layouts  1.57 us

profile of v2, /device:TPU:0, one launch (start us, length us, event | category | flops | bytes accessed | tf_op | source)
XLA Modules:
  0.0 55.8 jit_solution(3817275942706065274)
XLA Ops:
  0.0 54.2 %fold_and_butterfly.1 = f32[128,256]{1,0:T(8,128)} custom-call(f32[2,256,2048]{2,1,0:T(8,128)} %x_hbm.1, f32[64,32,512]{2,1,0:T(8,128)} %s_hbm.1, f32[3,256,1024]{2,1,0:T(8,128)} %w_hbm.1, f32[512,512]{1,0:T(8,128)} %e_hbm.1, bf16[2048,256]{1,0:T(8,128)(2,1)} %constant.4.clone.table_hi_hbm, bf16[2048,256]{1,0:T(8,128)(2,1)} %constant.5.clone.table_lo_hbm), custom_call_target="tpu_custom_call" | custom-call | tf_op jit(solution)/shard_map/fold_and_butterfly/pallas_call | solution.py:394
  54.2 1.6 %copy.8 = f32[128,256]{1,0:T(8,128)} copy(f32[128,256]{1,0:T(8,128)} %fold_and_butterfly.1) | data formatting | bytes 262144

commit v3 on v2

--- a/solution.py
+++ b/solution.py
@@ -300,11 +300,9 @@
         return 0
 
     lax.fori_loop(0, planes, gram, 0)
-    coeffs = turned(acc[:coeff_count], acc[coeff_count:], tau_dev)
-
-    for level in range(w_ref.shape[0]):
-        level_send[level] = coeffs
-        flip = 1 << level
+    level_send[0] = turned(acc[:coeff_count], acc[coeff_count:], tau_dev)
+
+    def apply_level(level, flip):
         partner = ti + (1 - 2 * (ti // flip % 2)) * flip
         exchange = pltpu.make_async_remote_copy(
             src_ref=level_send.at[level],
@@ -320,20 +318,27 @@
             columns = slice(block * coeff_count, (block + 1) * coeff_count)
             return dot_pairs((w_hi[level, :, columns], w_lo[level, :, columns]), pairs)
 
-        own = halves(coeffs)
+        own = halves(level_send[level])
         real_rows, imag_rows = part(0, own), part(2, own)
         exchange.wait()
         other = halves(level_recv[level])
-        coeffs = turned(real_rows + part(1, other), imag_rows + part(3, other), tau_dev)
-
-    pairs = halves(coeffs)
+        level_send[level + 1] = turned(
+            real_rows + part(1, other), imag_rows + part(3, other), tau_dev
+        )
+        return 2 * flip
+
+    levels = w_ref.shape[0]
+    lax.fori_loop(0, levels, apply_level, 1)
+    pairs = halves(level_send[levels])
     image = (
         dot_pairs((e_hi[:, :coeff_count], e_lo[:, :coeff_count]), pairs)[:, :tau_dev]
         - dot_pairs((e_hi[:, coeff_count:], e_lo[:, coeff_count:]), pairs)[:, tau_dev:]
     )
     rows_out = out_ref.shape[0]
     for f in range(freq_count):
-        image_send[f] = image[f * rows_out : (f + 1) * rows_out]
+        top = f * rows_out
+        middle, bottom = top + rows_out // 2, top + rows_out
+        image_send[f] = jnp.concatenate([image[top:middle], image[middle:bottom]], axis=1)
 
     def image_copy(target, source):
         return pltpu.make_async_remote_copy(
@@ -369,7 +374,11 @@
 
     lax.fori_loop(0, devices, wait_sent, 0)
     lax.fori_loop(1, freq_count, wait_image, 0)
-    out_ref[...] = jnp.concatenate([image_recv[f] for f in range(freq_count)], axis=1)
+    for part in range(2):
+        out_ref[part * rows_out // 2 : (part + 1) * rows_out // 2] = jnp.concatenate(
+            [image_recv[f, :, part * tau_dev : (part + 1) * tau_dev] for f in range(freq_count)],
+            axis=1,
+        )
 
 
 def fused(traces, source_weights, level_weights, slowness_weights):
@@ -412,10 +421,10 @@
             pltpu.VMEM(blocks + (shot_dev, box_offsets, width), f32),
             pltpu.VMEM(blocks + (shot_dev, box_offsets, width), f32),
             pltpu.VMEM((columns, width), f32),
+            pltpu.VMEM((levels + 1, coeff_count, width), f32),
             pltpu.VMEM((levels, coeff_count, width), f32),
-            pltpu.VMEM((levels, coeff_count, width), f32),
-            pltpu.VMEM((freq_count, rows_out, width // 2), f32),
-            pltpu.VMEM((freq_count, rows_out, width // 2), f32),
+            pltpu.VMEM((freq_count, rows_out // 2, width), f32),
+            pltpu.VMEM((freq_count, rows_out // 2, width), f32),
             dma((planes,)),
             dma((5,)),
             dma(blocks),

time: 55.9 us -> 55.1 us (0.986)
  Pallas kernels: 54.2 us -> 53.4 us
    pallas_call x1, Pallas kernels: 54.2 us -> 53.4 us  [fused(): pl.pallas_call(functools.partial(kernel, freq_count, trace_count), out_sh...]
where the time goes in v3:
time: 55.1 us; the launch traced here: 54.9 us
  Pallas kernels  53.4 us (97%)
  local copies, waits for them, and re-layouts  1.57 us (3%)
    pallas_call x1, Pallas kernels, fused(): pl.pallas_call(functools.partial(kernel, freq_count, trace_count), out_sh...  53.4 us
    unnamed x1, local copies, waits for them, and re-layouts  1.57 us

profile of v3, /device:TPU:0, one launch (start us, length us, event | category | flops | bytes accessed | tf_op | source)
XLA Modules:
  0.0 54.9 jit_solution(17449323951355011238)
XLA Ops:
  0.0 53.4 %fold_and_butterfly.1 = f32[128,256]{1,0:T(8,128)} custom-call(f32[2,256,2048]{2,1,0:T(8,128)} %x_hbm.1, f32[64,32,512]{2,1,0:T(8,128)} %s_hbm.1, f32[3,256,1024]{2,1,0:T(8,128)} %w_hbm.1, f32[512,512]{1,0:T(8,128)} %e_hbm.1, bf16[2048,256]{1,0:T(8,128)(2,1)} %constant.4.clone.table_hi_hbm, bf16[2048,256]{1,0:T(8,128)(2,1)} %constant.5.clone.table_lo_hbm), custom_call_target="tpu_custom_call" | custom-call | tf_op jit(solution)/shard_map/fold_and_butterfly/pallas_call | solution.py:403
  53.4 1.6 %copy.8 = f32[128,256]{1,0:T(8,128)} copy(f32[128,256]{1,0:T(8,128)} %fold_and_butterfly.1) | data formatting | bytes 262144

commit v4 on v3

--- a/solution.py
+++ b/solution.py
@@ -164,7 +164,7 @@
     lax.fori_loop(1, devices, greet, 0)
 
     def plane_at(turn):
-        return exclusive_or(my_plane, planes - 1 - turn, planes)
+        return exclusive_or(my_plane, (planes - 1 - turn) // 2 * 2 + turn % 2, planes)
 
     def load_x(turn):
         rows = pl.ds(pl.multiple_of(plane_at(turn) * plane_offsets, plane_offsets), plane_offsets)
@@ -242,7 +242,7 @@
             pl.semaphore_wait(barrier, devices - 1)
 
         def start(i, _):
-            f, core = (fi + i // CORES) % freq_count, i % CORES
+            f, core = exclusive_or(fi, freq_count - 1 - i // CORES, freq_count), i % CORES
 
             @pl.when(jnp.logical_not(is_me(plane, f, core)))
             def _():

time: 55.1 us -> 52.3 us (0.949)
  Pallas kernels: 53.4 us -> 50.6 us
    pallas_call x1, Pallas kernels: 53.4 us -> 50.6 us  [fused(): pl.pallas_call(functools.partial(kernel, freq_count, trace_count), out_sh...]
where the time goes in v4:
time: 52.3 us; the launch traced here: 52.2 us
  Pallas kernels  50.6 us (97%)
  local copies, waits for them, and re-layouts  1.57 us (3%)
    pallas_call x1, Pallas kernels, fused(): pl.pallas_call(functools.partial(kernel, freq_count, trace_count), out_sh...  50.6 us
    unnamed x1, local copies, waits for them, and re-layouts  1.57 us

profile of v4, /device:TPU:0, one launch (start us, length us, event | category | flops | bytes accessed | tf_op | source)
XLA Modules:
  0.0 52.2 jit_solution(9801485823455148192)
XLA Ops:
  0.0 50.6 %fold_and_butterfly.1 = f32[128,256]{1,0:T(8,128)} custom-call(f32[2,256,2048]{2,1,0:T(8,128)} %x_hbm.1, f32[64,32,512]{2,1,0:T(8,128)} %s_hbm.1, f32[3,256,1024]{2,1,0:T(8,128)} %w_hbm.1, f32[512,512]{1,0:T(8,128)} %e_hbm.1, bf16[2048,256]{1,0:T(8,128)(2,1)} %constant.4.clone.table_hi_hbm, bf16[2048,256]{1,0:T(8,128)(2,1)} %constant.5.clone.table_lo_hbm), custom_call_target="tpu_custom_call" | custom-call | tf_op jit(solution)/shard_map/fold_and_butterfly/pallas_call | solution.py:403
  50.6 1.6 %copy.8 = f32[128,256]{1,0:T(8,128)} copy(f32[128,256]{1,0:T(8,128)} %fold_and_butterfly.1) | data formatting | bytes 262144
